TPU v7x, 32 devices: a whole 2x2x4 slice. The times are simulated.
32 devices in a mesh: depth: 2 (over core), dp: 16 (over z, y, x).
Axes of the slice: x: 2, y: 2, z: 4, core: 2. Of those that a mesh axis runs over, the one named last changes fastest.
Arguments:
- inputs: bfloat16 [64, 512, 768], P(('depth', 'dp')), may hold values from -6 to 6
- output_gradient: bfloat16 [64, 512, 768], P(('depth', 'dp')), may hold values from -6 to 6
- keep: int32 [64], P(('depth', 'dp')), may hold values 0 or 1
- lengths: int32 [64], P(('depth', 'dp')), may hold values from 64 to 512
- routes: int32 [64], P(('depth', 'dp')), may hold values from 0 to 1
- attn_weights: float32 [256, 96, 96], P(('depth', 'dp'))
- attn_stats: float32 [256, 2, 96, 96], P(('depth', 'dp'))
- attn_roots: float32 [256, 2, 96, 96], P(('depth', 'dp'))
- attn_momentum: float32 [256, 96, 96], P(('depth', 'dp')), may hold values from -0.005859375 to 0.005859375
- ffn_weights: float32 [512, 96, 96], P(('depth', 'dp'))
- ffn_stats: float32 [512, 2, 96, 96], P(('depth', 'dp'))
- ffn_roots: float32 [512, 2, 96, 96], P(('depth', 'dp'))
- ffn_momentum: float32 [512, 96, 96], P(('depth', 'dp')), may hold values from -0.005859375 to 0.005859375
- vec_weights: float32 [9216], P(('depth', 'dp'))
- vec_first: float32 [9216], P(('depth', 'dp')), may hold values from -0.0012207031 to 0.0012207031
- vec_second: float32 [9216], P(('depth', 'dp')), may hold values from 5.644054e-10 to 2.2576216e-09
Outputs:
- out: bfloat16 [64, 512, 768], P(('depth', 'dp'))
- in_grad: bfloat16 [64, 512, 768], P(('depth', 'dp'))
- grad_norm: float32 [], replicated
- attn_stats_new: float32 [256, 2, 96, 96], P(('depth', 'dp'))
- attn_momentum_new: float32 [256, 96, 96], P(('depth', 'dp'))
- attn_weights_new: float32 [256, 96, 96], P(('depth', 'dp'))
- ffn_stats_new: float32 [512, 2, 96, 96], P(('depth', 'dp'))
- ffn_momentum_new: float32 [512, 96, 96], P(('depth', 'dp'))
- ffn_weights_new: float32 [512, 96, 96], P(('depth', 'dp'))
- vec_first_new: float32 [9216], P(('depth', 'dp'))
- vec_second_new: float32 [9216], P(('depth', 'dp'))
- vec_weights_new: float32 [9216], P(('depth', 'dp'))
All inputs are finite; a program needn't handle non-finite values. No bound on the sum of `keep` on one device may be relied on, other than what follows from the above.
Results may differ from a plain program's by a relative error of at most 0.012.
The roundings to bfloat16 on the way count: a program that leaves them out, or rounds other values in their place, can miss the bound.
Values may be sent and summed in bfloat16 or wider, within the bound.
A program may use at most 192 MiB of HBM per device.

v0:
```python
import functools
import math

import jax
import jax.numpy as jnp
from jax import lax
from jax.experimental import pallas as pl
from jax.experimental.pallas import tpu as pltpu
from jax.sharding import PartitionSpec as P

HEADS = 12
FF = 3072
BLOCK = 96
STEP = 10


norm_floor = 1e-05
masked_fill = -1000000000.0
momentum_decay = 0.9
stat_decay = 0.95
matrix_rate = 1.0
matrix_decay = 0.01
clip_bound = 1.0
first_decay = 0.9
second_decay = 0.999
vector_rate = 0.5
adam_floor = 1e-08


def serve_flags(keep_rows, route_rows):
    count = keep_rows.shape[-1]
    order = jnp.arange(count, dtype=jnp.int32)
    earlier = (order[None, :] < order[:, None]).astype(jnp.int32)
    same = (route_rows[:, :, None] == route_rows[:, None, :]).astype(jnp.int32)
    clash = jnp.sum(same * earlier[None, :, :] * keep_rows[:, None, :], axis=2)
    return keep_rows * (clash == 0).astype(jnp.int32)


def to_matrix(blocks, height, breadth):
    shaped = blocks.reshape(height // BLOCK, breadth // BLOCK, BLOCK, BLOCK)
    return shaped.transpose(0, 2, 1, 3).reshape(height, breadth)


def to_flat_blocks(matrix):
    height, breadth = matrix.shape
    shaped = matrix.reshape(height // BLOCK, BLOCK, breadth // BLOCK, BLOCK)
    return shaped.transpose(0, 2, 1, 3).reshape(-1, BLOCK * BLOCK)


def norm_parts(resid):
    center = resid - jnp.mean(resid, axis=-1, keepdims=True)
    factor = lax.rsqrt(jnp.mean(center * center, axis=-1, keepdims=True) + norm_floor)
    return (center * factor, factor)


def norm_back(grad_normed, normed, factor):
    middle = jnp.mean(grad_normed, axis=-1, keepdims=True)
    along = jnp.mean(grad_normed * normed, axis=-1, keepdims=True)
    return factor * (grad_normed - middle - normed * along)


def gelu_slope(value):
    cumulative = 0.5 * (1.0 + lax.erf(value * (1.0 / math.sqrt(2.0))))
    density = jnp.exp(-0.5 * value * value) * (1.0 / math.sqrt(2.0 * math.pi))
    return cumulative + value * density


def product(left, right):
    return jnp.dot(left, right, preferred_element_type=jnp.float32)


def contract_rows(left, right):
    return lax.dot_general(
        left, right, (((0,), (0,)), ((), ())), preferred_element_type=jnp.float32
    )


def times_transpose(left, right):
    return lax.dot_general(
        left, right, (((1,), (1,)), ((), ())), preferred_element_type=jnp.float32
    )


def masked_scores(query, keys, visible_len):
    scale = 1.0 / math.sqrt(query.shape[-1])
    scores = jnp.einsum("qhe,khe->hqk", query, keys, preferred_element_type=jnp.float32) * scale
    visible = jnp.arange(keys.shape[0], dtype=jnp.int32) < visible_len
    return jnp.where(visible[None, None, :], scores, masked_fill)


def attend_forward(pieces):
    query, keys, values, visible_len = pieces
    scores = masked_scores(query, keys, visible_len)
    peak = jnp.max(scores, axis=-1, keepdims=True)
    expo = jnp.exp(scores - peak)
    total = jnp.sum(expo, axis=-1, keepdims=True)
    probs_low = (expo / total).astype(jnp.bfloat16)
    context = jnp.einsum("hqk,khe->qhe", probs_low, values, preferred_element_type=jnp.float32)
    return (context, peak[..., 0] + jnp.log(total[..., 0]))


def attend_backward(pieces):
    query, keys, values, grad_ctx, log_total, visible_len = pieces
    scale = 1.0 / math.sqrt(query.shape[-1])
    scores = masked_scores(query, keys, visible_len)
    probs = jnp.exp(scores - log_total[..., None])
    probs_low = probs.astype(jnp.bfloat16)
    grad_probs = jnp.einsum("qhe,khe->hqk", grad_ctx, values, preferred_element_type=jnp.float32)
    grad_values = jnp.einsum(
        "hqk,qhe->khe", probs_low, grad_ctx, preferred_element_type=jnp.float32
    )
    along = jnp.sum(probs * grad_probs, axis=-1, keepdims=True)
    grad_scores = (probs * (grad_probs - along)).astype(jnp.bfloat16)
    grad_query = (
        jnp.einsum("hqk,khe->qhe", grad_scores, keys, preferred_element_type=jnp.float32) * scale
    )
    grad_keys = (
        jnp.einsum("hqk,qhe->khe", grad_scores, query, preferred_element_type=jnp.float32) * scale
    )
    return (grad_query, grad_keys, grad_values)


def shampoo(weights, stats, roots, momentum, grads, factor):
    highest = lax.Precision.HIGHEST
    clipped = grads * factor
    moment = momentum_decay * momentum + clipped
    left = jnp.einsum("nab,ncb->nac", clipped, clipped, precision=highest)
    right = jnp.einsum("nab,nac->nbc", clipped, clipped, precision=highest)
    fresh = stat_decay * stats + (1.0 - stat_decay) * jnp.stack([left, right], axis=1)
    turned = jnp.einsum("nab,nbc->nac", roots[:, 0], moment, precision=highest)
    turned = jnp.einsum("nab,nbc->nac", turned, roots[:, 1], precision=highest)
    updated = weights - matrix_rate * (turned + matrix_decay * weights)
    return (fresh, moment, updated)


def adam_step(weights, first, second, grads, factor):
    clipped = grads * factor
    first_new = first_decay * first + (1.0 - first_decay) * clipped
    second_new = second_decay * second + (1.0 - second_decay) * clipped * clipped
    first_hat = first_new / (1.0 - first_decay**STEP)
    second_hat = second_new / (1.0 - second_decay**STEP)
    updated = weights - vector_rate * first_hat / (jnp.sqrt(second_hat) + adam_floor)
    return (first_new, second_new, updated)


def per_device_general(
    inputs,
    output_gradient,
    keep,
    lengths,
    routes,
    attn_weights,
    attn_stats,
    attn_roots,
    attn_momentum,
    ffn_weights,
    ffn_stats,
    ffn_roots,
    ffn_momentum,
    vec_weights,
    vec_first,
    vec_second,
):
    slots, seq_len, width = inputs.shape
    tokens = slots * seq_len
    head_size = width // HEADS
    hidden_width = FF
    depth_count = lax.axis_size("depth")
    peer_slots = slots // depth_count
    grid = (width // BLOCK) ** 2
    half_ffn = width * hidden_width // (BLOCK * BLOCK)
    area = BLOCK * BLOCK
    low_type = jnp.bfloat16
    attn_flat = attn_weights.reshape(-1, area).astype(low_type)
    ffn_flat = ffn_weights.reshape(-1, area).astype(low_type)
    attn_all, ffn_all, vec_all = (
        lax.all_gather(attn_flat, ("depth", "dp"), axis=0, tiled=True),
        lax.all_gather(ffn_flat, ("depth", "dp"), axis=0, tiled=True),
        lax.all_gather(vec_weights.astype(low_type), ("depth", "dp"), axis=0, tiled=True),
    )
    table_keep, table_len, table_route = (
        lax.all_gather(keep, "depth", axis=0, tiled=True),
        lax.all_gather(lengths, "depth", axis=0, tiled=True),
        lax.all_gather(routes, "depth", axis=0, tiled=True),
    )
    mine = serve_flags(keep[None, :], routes[None, :])[0]
    slot_order = jnp.arange(slots, dtype=jnp.int32)
    selection = ((routes[None, :] == slot_order[:, None]).astype(jnp.int32) * mine[None, :]).astype(
        low_type
    )
    outgoing_rows = jnp.einsum(
        "gz,zrp->grp", selection, inputs, preferred_element_type=jnp.float32
    ).astype(low_type)
    send_grad = jnp.einsum(
        "gz,zrp->grp", selection, output_gradient, preferred_element_type=jnp.float32
    ).astype(low_type)
    come_rows, come_grad = (
        lax.all_to_all(outgoing_rows, "depth", split_axis=0, concat_axis=0, tiled=True),
        lax.all_to_all(send_grad, "depth", split_axis=0, concat_axis=0, tiled=True),
    )
    all_keep = table_keep.reshape(depth_count, slots)
    all_route = table_route.reshape(depth_count, slots)
    all_len = table_len.reshape(depth_count, slots)
    all_served = serve_flags(all_keep, all_route)
    here = lax.axis_index("depth")
    source = slot_order // peer_slots
    target = here * peer_slots + slot_order % peer_slots
    source_hot = (source[:, None] == jnp.arange(depth_count, dtype=jnp.int32)[None, :]).astype(
        jnp.int32
    )
    match = (all_route[None, :, :] == target[:, None, None]).astype(jnp.int32) * all_served[
        None, :, :
    ]
    slot_len = jnp.sum(source_hot[:, :, None] * match * all_len[None, :, :], axis=(1, 2))
    visible_len = jnp.maximum(slot_len, 1)
    query_w = to_matrix(attn_all[0:grid], width, width)
    key_w = to_matrix(attn_all[grid : 2 * grid], width, width)
    value_w = to_matrix(attn_all[2 * grid : 3 * grid], width, width)
    output_w = to_matrix(attn_all[3 * grid : 4 * grid], width, width)
    vectors = vec_all.astype(jnp.float32)
    q_bias = vectors[0:width]
    v_bias = vectors[width : 2 * width]
    out_bias = vectors[2 * width : 3 * width]
    hidden_bias = vectors[3 * width : 3 * width + hidden_width]
    ffn_bias = vectors[3 * width + hidden_width : 4 * width + hidden_width]
    gain_one = vectors[4 * width + hidden_width : 5 * width + hidden_width]
    shift_one = vectors[5 * width + hidden_width : 6 * width + hidden_width]
    gain_two = vectors[6 * width + hidden_width : 7 * width + hidden_width]
    shift_two = vectors[7 * width + hidden_width : 8 * width + hidden_width]
    flat = come_rows.reshape(tokens, width)
    four = (slots, seq_len, HEADS, head_size)
    query = (product(flat, query_w) + q_bias).astype(low_type).reshape(four)
    keys = product(flat, key_w).astype(low_type).reshape(four)
    values = (product(flat, value_w) + v_bias).astype(low_type).reshape(four)
    context, log_total = lax.map(attend_forward, (query, keys, values, visible_len))
    context_low = context.reshape(tokens, width).astype(low_type)
    attended = product(context_low, output_w) + out_bias
    normed_one, factor_one = norm_parts(flat.astype(jnp.float32) + attended)
    hidden_in = normed_one * gain_one + shift_one
    hidden_low = hidden_in.astype(low_type)
    hidden_w = to_matrix(ffn_all[0:half_ffn], width, hidden_width)
    return_weight = to_matrix(ffn_all[half_ffn:], hidden_width, width)
    before = product(hidden_low, hidden_w) + hidden_bias
    active_low = jax.nn.gelu(before, approximate=False).astype(low_type)
    branch = product(active_low, return_weight) + ffn_bias
    normed_two, factor_two = norm_parts(hidden_in + branch)
    result_low = (normed_two * gain_two + shift_two).astype(low_type)
    grad_rows = come_grad.reshape(tokens, width).astype(jnp.float32)
    grad_gain_two = jnp.sum(grad_rows * normed_two, axis=0)
    grad_shift_two = jnp.sum(grad_rows, axis=0)
    grad_resid_two = norm_back(grad_rows * gain_two, normed_two, factor_two)
    grad_branch = grad_resid_two.astype(low_type)
    grad_ffn_bias = jnp.sum(grad_branch.astype(jnp.float32), axis=0)
    gradient_return_weight = contract_rows(active_low, grad_branch)
    grad_active = times_transpose(grad_branch, return_weight)
    grad_before = (grad_active * gelu_slope(before)).astype(low_type)
    grad_hidden_bias = jnp.sum(grad_before.astype(jnp.float32), axis=0)
    grad_hidden_w = contract_rows(hidden_low, grad_before)
    grad_hidden = times_transpose(grad_before, hidden_w) + grad_resid_two
    grad_gain_one = jnp.sum(grad_hidden * normed_one, axis=0)
    grad_shift_one = jnp.sum(grad_hidden, axis=0)
    grad_resid_one = norm_back(grad_hidden * gain_one, normed_one, factor_one)
    ffn_grad = jnp.concatenate(
        [to_flat_blocks(grad_hidden_w), to_flat_blocks(gradient_return_weight)], axis=0
    )
    grad_attended = grad_resid_one.astype(low_type)
    grad_out_bias = jnp.sum(grad_attended.astype(jnp.float32), axis=0)
    grad_output_w = contract_rows(context_low, grad_attended)
    grad_context = times_transpose(grad_attended, output_w).astype(low_type).reshape(four)
    grad_query, grad_keys, grad_values = lax.map(
        attend_backward, (query, keys, values, grad_context, log_total, visible_len)
    )
    grad_query = grad_query.reshape(tokens, width).astype(low_type)
    grad_keys = grad_keys.reshape(tokens, width).astype(low_type)
    grad_values = grad_values.reshape(tokens, width).astype(low_type)
    grad_q_bias = jnp.sum(grad_query.astype(jnp.float32), axis=0)
    grad_v_bias = jnp.sum(grad_values.astype(jnp.float32), axis=0)
    grad_query_w = contract_rows(flat, grad_query)
    grad_key_w = contract_rows(flat, grad_keys)
    grad_value_w = contract_rows(flat, grad_values)
    in_rows = (
        grad_resid_one
        + times_transpose(grad_query, query_w)
        + times_transpose(grad_keys, key_w)
        + times_transpose(grad_values, value_w)
    )
    attn_grad = jnp.concatenate(
        [
            to_flat_blocks(grad_query_w),
            to_flat_blocks(grad_key_w),
            to_flat_blocks(grad_value_w),
            to_flat_blocks(grad_output_w),
        ],
        axis=0,
    )
    vec_grad = jnp.concatenate(
        [
            grad_q_bias,
            grad_v_bias,
            grad_out_bias,
            grad_hidden_bias,
            grad_ffn_bias,
            grad_gain_one,
            grad_shift_one,
            grad_gain_two,
            grad_shift_two,
        ]
    )
    attn_share, ffn_share, vec_share = (
        lax.psum_scatter(attn_grad, ("depth", "dp"), scatter_dimension=0, tiled=True),
        lax.psum_scatter(ffn_grad, ("depth", "dp"), scatter_dimension=0, tiled=True),
        lax.psum_scatter(vec_grad, ("depth", "dp"), scatter_dimension=0, tiled=True),
    )
    returned_rows, returned_gradient = (
        lax.all_to_all(
            result_low.reshape(slots, seq_len, width),
            "depth",
            split_axis=0,
            concat_axis=0,
            tiled=True,
        ),
        lax.all_to_all(
            in_rows.astype(low_type).reshape(slots, seq_len, width),
            "depth",
            split_axis=0,
            concat_axis=0,
            tiled=True,
        ),
    )
    stay = (1 - mine).astype(jnp.float32)[:, None, None]
    out = (
        jnp.einsum("rx,rmp->xmp", selection, returned_rows, preferred_element_type=jnp.float32)
        + stay * inputs.astype(jnp.float32)
    ).astype(low_type)
    in_grad = (
        jnp.einsum("rx,rmp->xmp", selection, returned_gradient, preferred_element_type=jnp.float32)
        + stay * output_gradient.astype(jnp.float32)
    ).astype(low_type)
    square = (
        jnp.sum(attn_share * attn_share)
        + jnp.sum(ffn_share * ffn_share)
        + jnp.sum(vec_share * vec_share)
    )
    total = lax.psum(square, ("depth", "dp"))
    grad_norm = jnp.sqrt(total)
    factor = clip_bound / jnp.maximum(grad_norm, clip_bound)
    attn_square = attn_share.reshape(-1, BLOCK, BLOCK)
    ffn_square = ffn_share.reshape(-1, BLOCK, BLOCK)
    attn_fresh, attn_moment, attn_updated = shampoo(
        attn_weights, attn_stats, attn_roots, attn_momentum, attn_square, factor
    )
    ffn_fresh, ffn_moment, ffn_updated = shampoo(
        ffn_weights, ffn_stats, ffn_roots, ffn_momentum, ffn_square, factor
    )
    first_new, second_new, vec_updated = adam_step(
        vec_weights, vec_first, vec_second, vec_share, factor
    )
    return (
        out,
        in_grad,
        grad_norm,
        attn_fresh,
        attn_moment,
        attn_updated,
        ffn_fresh,
        ffn_moment,
        ffn_updated,
        first_new,
        second_new,
        vec_updated,
    )


MESH = pl.DeviceIdType.MESH
BF = jnp.bfloat16
F32 = jnp.float32
LEN = 512
ROWS = 16


def place():
    d = lax.axis_index("depth")
    i = lax.axis_index("dp")
    x = i % 2
    y = (i // 2) % 2
    nx = i + 1 - 2 * x
    ny = i + 2 - 4 * y
    na = ny + d * (nx - ny)
    nb = nx + d * (ny - nx)
    return dict(d=d, i=i, z=i // 4, c=i % 4, na=na, nb=nb, ca=na % 4, cb=nb % 4, cd=3 - i % 4)


def near(p):
    peers = [(p["d"], p["na"]), (p["d"], p["nb"]), (1 - p["d"], p["i"])]
    return peers + [(p["d"], ((p["z"] + k) % 4) * 4 + p["c"]) for k in (1, 2, 3)]


def greet(peers):
    barrier = pltpu.get_barrier_semaphore()
    for peer in peers:
        pl.semaphore_signal(barrier, inc=1, device_id=peer, device_id_type=MESH)


def meet(peers):
    pl.semaphore_wait(pltpu.get_barrier_semaphore(), len(peers))


def remote(src, dst, send, recv, k, dev):
    return pltpu.make_async_remote_copy(src_ref=src, dst_ref=dst, send_sem=send.at[k], recv_sem=recv.at[k],
                                        device_id=dev, device_id_type=MESH)


class Mail:
    def __init__(self, p, send, recv):
        self.p, self.send, self.recv, self.sent = p, send, recv, []

    def go(self, src, dst, k, dev):
        copy = remote(src, dst, self.send, self.recv, k, dev)
        copy.start()
        self.sent.append(copy)

    def wait(self, dst, k):
        remote(dst, dst, self.send, self.recv, k, (self.p["d"], self.p["na"])).wait_recv()

    def drain(self):
        for copy in self.sent:
            copy.wait_send()


class Spread:
    def __init__(self, p, a, b, to_a, to_b, own, slot, column, send, recv, local):
        d, z, i, c = p["d"], p["z"], p["i"], p["c"]
        ca, cb = a % 4, b % 4
        self.keep = pltpu.make_async_copy(own, slot(d, z, c), local)
        lines = [(own, slot(d, z, c), (d, ((z + k) % 4) * 4 + c)) for k in (1, 2, 3)]
        takes = [slot(d, (z + 4 - k) % 4, c) for k in (1, 2, 3)]
        mine, from_a, from_b, far = (column(d, col) for col in (c, ca, cb, p["cd"]))
        core = (1 - d, i)
        sends = [(mine, 3, (d, a)), (mine, 4, (d, b)), (from_a, 5, (d, b)), (mine, 6, core), (from_a, to_a, core),
                 (from_b, to_b, core), (far, 9, core)]
        self.lines = [remote(src, dst, send, recv, k, dev) for k, (src, dst, dev) in enumerate(lines)]
        self.taken = [remote(dst, dst, send, recv, k, (d, a)) for k, dst in enumerate(takes)]
        self.sends = [remote(src, src, send, recv, k, dev) for src, k, dev in sends]
        waits = [(from_a, 3), (from_b, 4), (far, 5), (column(1 - d, c), 6), (column(1 - d, ca), to_a),
                 (column(1 - d, cb), to_b), (column(1 - d, p["cd"]), 9)]
        self.came = [remote(dst, dst, send, recv, k, (d, a)) for dst, k in waits]

    def push(self, *which):
        for n in which:
            self.sends[n].start()

    def start(self):
        self.keep.start()
        for k in (1, 0, 2):
            self.lines[k].start()

    def second(self):
        self.keep.wait()
        for copy in self.taken:
            copy.wait_recv()
        self.push(0, 1, 3)

    def third(self):
        self.came[0].wait_recv()
        self.push(2, 4)

    def fourth(self):
        self.came[1].wait_recv()
        self.push(5)

    def fifth(self):
        self.came[2].wait_recv()
        self.push(6)

    def sixth(self):
        for copy in self.came[3:]:
            copy.wait_recv()

    def drain(self):
        for copy in self.lines + self.sends:
            copy.wait_send()


def spread_sems():
    return [pltpu.SemaphoreType.DMA((10,)), pltpu.SemaphoreType.DMA((10,)), pltpu.SemaphoreType.DMA]


def on_core(p, core, *steps):
    @pl.when(p["d"] == core)
    def _():
        for s in steps:
            s()


def at_step(m, value, *steps):
    @pl.when(m == value)
    def _():
        for s in steps:
            s()


def square_links(p):
    dx = p["i"] + 1 - 2 * (p["i"] % 2)
    dy = p["i"] + 2 - 4 * ((p["i"] // 2) % 2)
    return dx, dy


def quarter(w, q):
    return w.at[q // 2, pl.ds(2 * (q % 2), 2)]


def one_hot(shape, row, col):
    r = lax.broadcasted_iota(jnp.int32, shape, 0)
    c = lax.broadcasted_iota(jnp.int32, shape, 1)
    return (row(r) == col(c)).astype(F32)


def unfold_vec(pieces, vec, share):
    per = share // BLOCK
    stack = pieces[...][:, :, :, 0, :].reshape(32, pieces.shape[-1])
    units = sum(
        jnp.dot(one_hot((32 * per, 32), lambda u: u, lambda k, a=a: per * k + a), stack[:, a * BLOCK:(a + 1) * BLOCK],
                preferred_element_type=F32)
        for a in range(per)
    )
    for b in range(8):
        vec[:, b * BLOCK:(b + 1) * BLOCK] = jnp.dot(
            one_hot((ROWS, 32 * per), lambda r, b=b: 8 * r + b, lambda u: u), units, preferred_element_type=F32)


def dot_nn(a, b):
    return lax.dot_general(a, b, (((1,), (0,)), ((), ())), preferred_element_type=F32)


def dot_nt(a, b):
    return lax.dot_general(a, b, (((1,), (1,)), ((), ())), preferred_element_type=F32)


def dot_tn(a, b):
    return lax.dot_general(a, b, (((0,), (0,)), ((), ())), preferred_element_type=F32)


def square_of(value):
    return value.reshape(value.shape[0] * value.shape[1] * value.shape[2], value.shape[3])


def seq_rows(s):
    return pl.ds(s * LEN, LEN) if isinstance(s, int) else pl.ds(pl.multiple_of(s * LEN, LEN), LEN)


def tile_rows(s, size):
    return pl.ds(pl.multiple_of(s * size, size), size)


def served_flag(keep, routes, s):
    other = keep[0] * (routes[0] == routes[1]).astype(jnp.int32)
    return jnp.where(s == 0, keep[0], keep[1] * (1 - other))


def projections(x, ga, vec, q, k, v):
    width = x.shape[1]

    def tile(s, carry):
        rows = seq_rows(s)
        xr = x[rows]
        q[rows] = (dot_nn(xr, square_of(ga[0, 0:2])) + vec[0:1]).astype(BF)
        k[rows] = dot_nn(xr, square_of(ga[0, 2:4])).astype(BF)
        v[rows] = (dot_nn(xr, square_of(ga[1, 0:2])) + vec[1:2]).astype(BF)
        return carry

    lax.fori_loop(0, x.shape[0] // LEN, tile, 0)


def head_pairs(n, lens):
    s, g = n // 6, n % 6
    first = lax.broadcasted_iota(jnp.int32, (1, 128), 1) < 64
    return s, seq_rows(s), pl.ds(pl.multiple_of(g * 128, 128), 128), (first, jnp.logical_not(first))


def attend(n, q, k, v, lens, context, log_total):
    s, rows, cols, halves = head_pairs(n, lens)
    qp, kp, vp = q[rows, cols], k[rows, cols], v[rows, cols]
    seen = lax.broadcasted_iota(jnp.int32, (1, LEN), 1) < lens[s]
    found = []
    for h in range(2):
        qm = jnp.where(halves[h], qp, jnp.zeros_like(qp))
        scores = jnp.where(seen, dot_nt(qm, kp) * 0.125, masked_fill)
        peak = jnp.max(scores, axis=1, keepdims=True)
        expo = jnp.exp(scores - peak)
        total = jnp.sum(expo, axis=1, keepdims=True)
        found.append(dot_nn((expo * (1.0 / total)).astype(BF), vp))
        log_total[n, h] = (peak + jnp.log(total))[:, 0]
    context[rows, cols] = jnp.where(halves[0], found[0], found[1]).astype(BF)


def attend_back(n, q, k, v, grad_context, log_total, lens, gq, gk, gv):
    s, rows, cols, halves = head_pairs(n, lens)
    kp, vp = k[rows, cols], v[rows, cols]
    seen = lax.broadcasted_iota(jnp.int32, (LEN, 1), 0) < lens[s]
    ak = av = jnp.zeros((LEN, 128), F32)
    size = LEN // 2
    for t in range(2):
        part = tile_rows(2 * s + t, size)
        qp, gp = q[part, cols], grad_context[part, cols]
        aq = jnp.zeros((size, 128), F32)
        for h in range(2):
            qm, km, gm = (jnp.where(halves[h], t, jnp.zeros_like(t)) for t in (qp, kp, gp))
            scores = jnp.where(seen, dot_nt(kp, qm) * 0.125, masked_fill)
            probs = jnp.exp(scores - log_total[n, h][None, t * size:(t + 1) * size])
            grad_probs = dot_nt(vp, gm)
            along = jnp.sum(probs * grad_probs, axis=0, keepdims=True)
            grad_scores = (probs * (grad_probs - along)).astype(BF)
            av += dot_nn(probs.astype(BF), gm)
            ak += dot_nn(grad_scores, qm)
            aq += dot_tn(grad_scores, km)
        gq[part, cols] = (aq * 0.125).astype(BF)
    gk[rows, cols] = (ak * 0.125).astype(BF)
    gv[rows, cols] = av.astype(BF)


def mean_of(t):
    return jnp.mean(t, axis=-1, keepdims=True)


def attention_end(x, context, ga, vec, normed, factor):
    width = x.shape[1]

    def tile(s, carry):
        rows = seq_rows(s)
        attended = dot_nn(context[rows], square_of(ga[1, 2:4])) + vec[2:3]
        resid = x[rows].astype(F32) + attended
        center = resid - mean_of(resid)
        scale = lax.rsqrt(mean_of(center * center) + norm_floor)
        normed[rows] = center * scale
        factor[rows] = scale
        return carry

    lax.fori_loop(0, x.shape[0] // LEN, tile, 0)


def vec_part(vec, n):
    return vec[n:n + 1]


def input_gradient(x, cot, ga, grad_resid, keep, routes, gq, gk, gv, in_grad):
    def tile(s, carry):
        rows = tile_rows(s, LEN // 2)
        total = grad_resid[rows] + dot_nt(gq[rows], square_of(ga[0, 0:2]))
        total += dot_nt(gk[rows], square_of(ga[0, 2:4]))
        total += dot_nt(gv[rows], square_of(ga[1, 0:2]))
        in_grad[rows] = jnp.where(served_flag(keep, routes, s // 2) > 0, total.astype(BF), cot[rows])
        return carry

    lax.fori_loop(0, 2 * x.shape[0] // LEN, tile, 0)


def gather_attention_kernel(aw, fw, vw, x, lens, gf, ga_out, vec, q_out, k_out, v_out, context_out, log_total, normed_out, factor,
                            active_out, slope_out,
                            ga, gv, strip, pair, own, q, k, v, context, normed, low, w1, active, slope, store, wload, *sems):
    p = place()
    peers = near(p)
    greet(peers)
    share = vw.shape[0]
    own[...] = jnp.zeros_like(own)
    own[0:1, 0:share] = vw[...].astype(BF).astype(F32).reshape(1, share)
    for b in range(8):
        strip[:, b * BLOCK:(b + 1) * BLOCK] = aw[b].astype(BF)
    for j in range(2):
        for b in range(8):
            pair[j, :, b * BLOCK:(b + 1) * BLOCK] = fw[8 * j + b].astype(BF)
    half = BLOCK // 2
    seqs = x.shape[0] // LEN
    dx, dy = square_links(p)
    both = (p["na"], p["nb"], 8 - p["d"], 7 + p["d"])

    def attn_part(h):
        rows = pl.ds(h * half, half)
        return both + (strip.at[rows], lambda d, z, c: ga.at[d, z, c, rows], lambda d, c: ga.at[d, :, c, rows])

    def feed_part(j):
        links = (dy, dx, 8, 7) if j == 0 else (dx, dy, 7, 8)
        return links + (pair.at[j], lambda d, z, c: gf.at[d, z, c, j], lambda d, c: gf.at[d, :, c, j])

    vec_piece = both + (own, lambda d, z, c: gv.at[d, z, c], lambda d, c: gv.at[d, :, c])
    parts = [attn_part(0), vec_piece, attn_part(1), feed_part(0), feed_part(1)]
    a0, w, a1, f0, f1 = every = [Spread(p, *part, *sems[3 * n:3 * n + 3]) for n, part in enumerate(parts)]
    meet(peers)
    for s in (a0, w, a1):
        s.start()
    on_core(p, 0, f0.start, f1.start)
    a0.second()
    w.second()
    a1.second()
    for s in (a0, w, a1):
        s.third()
        s.fourth()
    on_core(p, 0, f0.second, f1.second)
    on_core(p, 1, f0.start, f1.start)
    for s in (a0, w, a1):
        s.fifth()
    w.sixth()
    unfold_vec(gv, vec, share)
    a0.sixth()
    a1.sixth()
    stores = [pltpu.make_async_copy(src, dst, store.at[n])
              for n, (src, dst) in enumerate(((q, q_out), (k, k_out), (v, v_out), (context, context_out), (normed, normed_out),
                                              (ga, ga_out)))]
    stores[5].start()
    projections(x, ga, vec, q, k, v)
    for copy in stores[:3]:
        copy.start()

    def step(n, carry):
        attend(n, q, k, v, lens, context, log_total)
        at_step(n, 3, lambda: on_core(p, 0, f0.third, f1.third, f0.fourth, f1.fourth))
        at_step(n, 4, lambda: on_core(p, 1, f0.second, f1.second))
        at_step(n, 9, lambda: on_core(p, 0, f0.fifth, f1.fifth))
        return carry

    lax.fori_loop(0, 12, step, 0)
    stores[3].start()
    attention_end(x, context, ga, vec, normed, factor)
    stores[4].start()
    on_core(p, 1, f0.sixth, f1.sixth)

    def fetch(t, carry):
        n, s = t // 8, t % 8
        pltpu.make_async_copy(gf.at[0, s // 2, 2 * (s % 2) + n // 2, n % 2], w1.at[n // 2, 2 * (n % 2) + s // 4, s % 4],
                              wload.at[n]).start()
        return carry

    lax.fori_loop(0, 32, fetch, 0)

    def lower(s, carry):
        rows = seq_rows(s)
        low[rows] = (normed[rows] * vec_part(vec, 8) + vec_part(vec, 9)).astype(BF)
        return carry

    lax.fori_loop(0, seqs, lower, 0)

    def enter(n, carry):
        pltpu.make_async_copy(quarter(w1, n), quarter(w1, n), wload.at[n]).wait()

        def tile(s, inner):
            rows = seq_rows(s)
            before = dot_nn(low[rows], square_of(quarter(w1, n)[...])) + vec[pl.ds(3 + n, 1)]
            cumulative = 0.5 * (1.0 + lax.erf(before * (1.0 / math.sqrt(2.0))))
            active[n, rows] = (before * cumulative).astype(BF)
            density = jnp.exp(-0.5 * before * before) * (1.0 / math.sqrt(2.0 * math.pi))
            slope[n, rows] = (cumulative + before * density).astype(BF)
            return inner

        lax.fori_loop(0, seqs, tile, 0)
        pltpu.make_async_copy(active.at[n], active_out.at[n], store.at[6 + n]).start()
        pltpu.make_async_copy(slope.at[n], slope_out.at[n], store.at[10 + n]).start()
        at_step(n, 1, lambda: on_core(p, 1, f0.third, f1.third, f0.fourth, f1.fourth))
        return carry

    lax.fori_loop(0, 4, enter, 0)
    on_core(p, 1, f0.fifth, f1.fifth)
    on_core(p, 0, f0.sixth, f1.sixth)
    for s in every:
        s.drain()
    for copy in stores:
        copy.wait()
    for n in range(4):
        pltpu.make_async_copy(active.at[n], active_out.at[n], store.at[6 + n]).wait()
        pltpu.make_async_copy(slope.at[n], slope_out.at[n], store.at[10 + n]).wait()


def gather_attention(aw, fw, vw, x, lens):
    tokens, width = x.shape
    low = jax.ShapeDtypeStruct(x.shape, BF)
    four = jax.ShapeDtypeStruct((4, tokens, width), BF)
    outs = [jax.ShapeDtypeStruct((2, 4, 4, 2, BLOCK, width), BF), jax.ShapeDtypeStruct((2, 4, 4, BLOCK, width), BF),
            jax.ShapeDtypeStruct((ROWS, width), F32)] + [low] * 4
    outs += [jax.ShapeDtypeStruct((12, 2, LEN), F32), jax.ShapeDtypeStruct(x.shape, F32),
             jax.ShapeDtypeStruct((tokens, 1), F32), four, four]
    vmem = pl.BlockSpec(memory_space=pltpu.VMEM)
    hbm = pl.BlockSpec(memory_space=pl.ANY)
    strips = pltpu.VMEM((2, 4, 4, BLOCK, width), BF)
    rows = pltpu.VMEM(x.shape, BF)
    wide = pltpu.VMEM((4, tokens, width), BF)
    return pl.pallas_call(
        gather_attention_kernel,
        out_shape=outs,
        in_specs=[vmem] * 4 + [pl.BlockSpec(memory_space=pltpu.SMEM)],
        out_specs=[hbm, hbm, vmem] + [hbm] * 4 + [vmem, hbm, vmem, hbm, hbm],
        scratch_shapes=[strips, pltpu.VMEM((2, 4, 4, 8, 384), F32), pltpu.VMEM((BLOCK, width), BF),
                        pltpu.VMEM((2, BLOCK, width), BF), pltpu.VMEM((8, 384), F32)]
        + [rows] * 4 + [pltpu.VMEM(x.shape, F32), rows, strips, wide, wide,
                        pltpu.SemaphoreType.DMA((14,)), pltpu.SemaphoreType.DMA((4,))]
        + spread_sems() * 5,
        compiler_params=pltpu.CompilerParams(collective_id=0, has_side_effects=True, vmem_limit_bytes=62 << 20),
        name="gather_attention",
    )(aw, fw, vw, x, lens)


def fold_scratch(width):
    shape = (BLOCK, width)
    return [pltpu.VMEM((4, 4) + shape, BF), pltpu.VMEM((4,) + shape, BF), pltpu.VMEM((4,) + shape, BF),
            pltpu.VMEM((4,) + shape, BF), pltpu.VMEM((3,) + shape, BF),
            pltpu.SemaphoreType.DMA((7,)), pltpu.SemaphoreType.DMA((7,))]


class Total(Mail):
    def __init__(self, p, held, came, send, recv):
        Mail.__init__(self, p, send, recv)
        self.held, self.came = held, came
        self.peers = ((1 - p["d"], p["i"]), (p["d"], p["na"]), (p["d"], p["nb"]))

    def start(self):
        self.go(self.held.at[0], self.came.at[0], 0, self.peers[0])

    def hop(self, n):
        p = self.p
        self.wait(self.came.at[n], n)
        self.held[n + 1] = self.held[n] + self.came[n]
        if n < 2:
            self.go(self.held.at[n + 1], self.came.at[n + 1], n + 1, self.peers[n + 1])
        else:
            for k in (1, 2, 3):
                self.go(self.held.at[3], self.came.at[2 + k], 2 + k, (p["d"], ((p["z"] + k) % 4) * 4 + p["c"]))

    def end(self):
        total = self.held[3]
        for k in (1, 2, 3):
            self.wait(self.came.at[2 + k], 2 + k)
            total += self.came[2 + k]
        return total


def own_share(p, rows, out, share):
    per = share // BLOCK
    me = p["d"] * 16 + p["i"]
    units = sum(
        jnp.dot(one_hot((8, ROWS), lambda a: per * me + jnp.where(a < per, a, -8 * 32 * per), lambda r, b=b: 8 * r + b),
                rows[:, b * BLOCK:(b + 1) * BLOCK], precision=lax.Precision.HIGHEST, preferred_element_type=F32)
        for b in range(8)
    )
    for a in range(per):
        out[0:1, a * BLOCK:(a + 1) * BLOCK] = units[a:a + 1]


def everyone(p):
    me = p["d"] * 16 + p["i"]

    def other(k):
        t = (me + k) % 32
        return (t // 16, t % 16)

    return me, other


def greet_all(p):
    me, other = everyone(p)
    barrier = pltpu.get_barrier_semaphore()

    def one(k, carry):
        pl.semaphore_signal(barrier, inc=1, device_id=other(k), device_id_type=MESH)
        return carry

    lax.fori_loop(1, 32, one, 0)


def meet_all():
    pl.semaphore_wait(pltpu.get_barrier_semaphore(), 31)


def norm_sum(p, square, slots, send, recv):
    me, other = everyone(p)
    slots[me] = jnp.full((8, 128), square, F32)
    to = lambda k, slot: remote(slots.at[slot], slots.at[slot], send, recv, slot, other(k))

    def push(k, carry):
        remote(slots.at[me], slots.at[me], send.at[pl.ds(k, 1)], recv.at[pl.ds(me, 1)], 0, other(k)).start()
        return carry

    def take(k, carry):
        slot = (me + k) % 32
        remote(slots.at[slot], slots.at[slot], send.at[pl.ds(k, 1)], recv.at[pl.ds(slot, 1)], 0, other(k)).wait_recv()
        return carry

    def done(k, carry):
        remote(slots.at[me], slots.at[me], send.at[pl.ds(k, 1)], recv.at[pl.ds(me, 1)], 0, other(k)).wait_send()
        return carry

    lax.fori_loop(1, 32, push, 0)
    lax.fori_loop(1, 32, take, 0)
    total = jnp.sum(slots[...], axis=0)[0:1, 0:1]
    lax.fori_loop(1, 32, done, 0)
    return total


class Fold:
    def __init__(self, p, a, b, away, home, pair, diag, flat, late, line, send, recv):
        self.p, self.home, self.pair, self.diag, self.flat, self.late, self.line = p, home, pair, diag, flat, late, line
        self.ca, self.cb = a % 4, b % 4
        d, z, c = p["d"], p["z"], p["c"]
        pieces = [(away, pair, (1 - d, p["i"])), (pair.at[:, p["cd"]], diag, (d, b)), (pair.at[:, self.cb], flat, (d, b)),
                  (pair.at[:, self.ca], late, (d, a))]
        pieces += [(pair.at[(z + k) % 4, c], line.at[k - 1], (d, ((z + k) % 4) * 4 + c)) for k in (1, 2, 3)]
        self.copies = [remote(src, dst, send, recv, n, dev) for n, (src, dst, dev) in enumerate(pieces)]

    def add(self, dst, *others):
        total = dst[...].astype(F32)
        for o in others:
            total += o[...].astype(F32)
        dst[...] = total.astype(dst.dtype)

    def start(self):
        self.copies[0].start()

    def second(self):
        self.copies[0].wait_recv()
        for col, n in ((self.p["cd"], 1), (self.cb, 2)):
            self.add(self.pair.at[:, col], self.home.at[:, col])
            self.copies[n].start()
        for col in (self.ca, self.p["c"]):
            self.add(self.pair.at[:, col], self.home.at[:, col])

    def third(self):
        self.copies[1].wait_recv()
        self.add(self.pair.at[:, self.ca], self.diag)
        self.copies[3].start()

    def fourth(self):
        p = self.p
        self.copies[2].wait_recv()
        self.copies[3].wait_recv()
        for k in (2, 1, 3, 0):
            dst = (p["z"] + k) % 4
            self.add(self.pair.at[dst, p["c"]], self.flat.at[dst], self.late.at[dst])
            if k:
                self.copies[3 + k].start()

    def fifth(self, out):
        p = self.p
        total = self.pair[p["z"], p["c"]].astype(F32)
        for k in (1, 2, 3):
            self.copies[3 + k].wait_recv()
            total += self.line[k - 1].astype(F32)
        out[...] = total

    def drain(self):
        for copy in self.copies:
            copy.wait_send()


def layer_back_kernel(x_in, cot_in, normed_in, active_in, slope_in, factor, gf, ga, q_in, k_in, v_in, context_in, log_total, vec, lens, keep, routes,
                      out, in_grad, sf, sa, sv, norm,
                      x, cot, normed, middle, low, grad_low, image, w1, w2, active, slope, hf, gvec, held, came, slots,
                      load, wload, nsend, nrecv, tsend, trecv, *scratch):
    p = place()
    greet_all(p)
    tokens, width = x.shape
    seqs = tokens // LEN
    half = width // 2
    lanes = (pl.ds(0, half), pl.ds(half, half))

    def bring(src, dst, n):
        return pltpu.make_async_copy(src, dst, load.at[n])

    ahead = [bring(active_in, active, 0), bring(normed_in, normed, 1), bring(x_in, x, 2), bring(cot_in, cot, 9)]
    slopes = bring(slope_in, slope, 10)

    def fetch_down(t, carry):
        q, s = t // 8, t % 8
        pltpu.make_async_copy(gf.at[1, q, s // 2, s % 2], w2.at[q // 2, 2 * (q % 2) + s // 4, s % 4], wload.at[0]).start()
        return carry

    def fetch(t, carry):
        q, s = t // 8, t % 8
        pltpu.make_async_copy(gf.at[0, s // 2, 2 * (s % 2) + q // 2, q % 2], w1.at[q // 2, 2 * (q % 2) + s // 4, s % 4],
                              wload.at[1]).start()
        return carry

    ahead[0].start()
    lax.fori_loop(0, 32, fetch_down, 0)
    for copy in ahead[1:]:
        copy.start()
    slopes.start()
    lax.fori_loop(0, 32, fetch, 0)
    dx, dy = square_links(p)
    f0 = Fold(p, dy, dx, hf.at[1 - p["d"], :, :, 0], hf.at[p["d"], :, :, 0], *scratch[0:7])
    f1 = Fold(p, dx, dy, hf.at[1 - p["d"], :, :, 1], hf.at[p["d"], :, :, 1], *scratch[7:14])
    ha, ga_in = w1, w2
    a0, a1 = [Fold(p, p["na"], p["nb"], ha.at[1 - p["d"], :, :, :, lanes[n]], ha.at[p["d"], :, :, :, lanes[n]],
                   *scratch[14 + 7 * n:21 + 7 * n]) for n in range(2)]
    total = Total(p, held, came, tsend, trecv)

    def on(core, *steps):
        on_core(p, core, *steps)

    gvec[...] = jnp.zeros_like(gvec)

    def add_vec(n, value):
        gvec[n:n + 1] += value

    def lower(s, carry):
        rows = seq_rows(s)
        low[rows] = (normed[rows] * vec_part(vec, 8) + vec_part(vec, 9)).astype(BF)
        return carry

    for copy in ahead[1:2]:
        copy.wait()
    lax.fori_loop(0, seqs, lower, 0)
    pltpu.make_async_copy(w2, w2, wload.at[0]).wait()
    for copy in ahead[:1] + ahead[2:]:
        copy.wait()
    tile = LEN // 2

    def leave(t, carry):
        rows = tile_rows(t, tile)
        show = pltpu.make_async_copy(image, out.at[rows], load.at[3])
        branch = dot_nn(active[0, rows], square_of(quarter(w2, 0)[...]))
        for q in range(1, 4):
            branch += dot_nn(active[q, rows], square_of(quarter(w2, q)[...]))
        resid = normed[rows] * vec_part(vec, 8) + vec_part(vec, 9) + (branch + vec_part(vec, 7))
        center = resid - mean_of(resid)
        scale = lax.rsqrt(mean_of(center * center) + norm_floor)
        second = center * scale
        served = served_flag(keep, routes, t // 2) > 0
        result = second * vec_part(vec, 10) + vec_part(vec, 11)
        image[...] = jnp.where(served, result.astype(BF), x[rows])
        show.start()
        grad = jnp.where(served, cot[rows].astype(F32), 0.0)
        add_vec(10, jnp.sum(grad * second, axis=0, keepdims=True))
        add_vec(11, jnp.sum(grad, axis=0, keepdims=True))
        grad = grad * vec_part(vec, 10)
        grad = scale * (grad - mean_of(grad) - second * mean_of(grad * second))
        middle[rows] = grad
        grad_low[rows] = grad.astype(BF)
        add_vec(7, jnp.sum(grad.astype(BF).astype(F32), axis=0, keepdims=True))
        show.wait()
        return carry

    lax.fori_loop(0, 2 * seqs, leave, 0)
    def down_grad(t, carry):
        q, h = t // 2, t % 2
        found = dot_tn(active[q, :, pl.ds(pl.multiple_of(h * half, half), half)], grad_low[...])
        hf[1, q, pl.ds(2 * h, 2)] = found.astype(BF).reshape(2, 2, BLOCK, width)
        return carry

    lax.fori_loop(0, 8, down_grad, 0)
    meet_all()
    on(0, f0.start, f1.start)
    again = [bring(src, slope.at[n], 4 + n) for n, src in enumerate((context_in, q_in, k_in, v_in))]
    context, qs, ks, vs = (slope.at[n] for n in range(4))
    slopes.wait()

    def turn(q, carry):
        def part(s, inner):
            rows = seq_rows(s)
            back = dot_nt(grad_low[rows], square_of(quarter(w2, q)[...])) * slope[q, rows].astype(F32)
            active[q, rows] = back.astype(BF)
            gvec[pl.ds(3 + q, 1)] += jnp.sum(back.astype(BF).astype(F32), axis=0, keepdims=True)
            return inner

        def up_grad(h, inner):
            found = dot_tn(low[:, pl.ds(pl.multiple_of(h * half, half), half)], active[q]).astype(BF).reshape(2, 2, BLOCK, width)
            for y in range(2):
                hf[0, pl.ds(2 * h, 2), 2 * y + q // 2, q % 2] = found[:, y]
            return inner

        lax.fori_loop(0, seqs, part, 0)
        lax.fori_loop(0, 2, up_grad, 0)
        at_step(q, 1, lambda: on(1, f0.second))
        at_step(q, 2, lambda: on(1, f1.second))
        return carry

    lax.fori_loop(0, 4, turn, 0)
    for copy in again:
        copy.start()
    pltpu.make_async_copy(w1, w1, wload.at[1]).wait()
    square_in = bring(ga, ga_in, 8)
    square_in.start()
    on(1, f0.start, f1.start)

    def close(t, carry):
        rows = tile_rows(t, tile)
        grad = middle[rows]
        for q in range(4):
            grad += dot_nt(active[q, rows], square_of(quarter(w1, q)[...]))
        head = normed[rows]
        add_vec(8, jnp.sum(grad * head, axis=0, keepdims=True))
        add_vec(9, jnp.sum(grad, axis=0, keepdims=True))
        grad = grad * vec_part(vec, 8)
        grad = factor[rows] * (grad - mean_of(grad) - head * mean_of(grad * head))
        middle[rows] = grad
        grad_low[rows] = grad.astype(BF)
        return carry

    lax.fori_loop(0, seqs, close, 0)
    on(1, f0.third)
    lax.fori_loop(seqs, 2 * seqs, close, 0)
    on(1, f1.third)
    on(0, f0.second)
    gq, gk, gv, grad_context = (active.at[n] for n in range(4))
    square_in.wait()
    again[0].wait()

    def open_attention(s, carry):
        rows = seq_rows(s)
        grad_context[rows] = dot_nt(grad_low[rows], square_of(ga_in[1, 2:4])).astype(BF)
        return carry

    lax.fori_loop(0, seqs, open_attention, 0)
    held[0] = gvec[...]
    held[0, 2:3] = jnp.sum(grad_low[...].astype(F32), axis=0, keepdims=True)
    for h in range(2):
        ha[1, 2 + h] = dot_tn(context[:, h * half:(h + 1) * half], grad_low[...]).astype(BF).reshape(4, BLOCK, width)
    on(0, f1.second)
    for copy in again[1:]:
        copy.wait()

    def step(m, carry):
        n = ((m % 6) // 3) * 6 + (m // 6) * 3 + m % 3
        attend_back(n, qs, ks, vs, grad_context, log_total, lens, gq, gk, gv)
        at_step(m, 1, lambda: on(1, f0.fourth))
        at_step(m, 2, lambda: on(1, f1.fourth))
        at_step(m, 3, lambda: on(0, f0.third))
        at_step(m, 4, lambda: on(0, f1.third))
        at_step(m, 5, lambda: weight_grads(0), a0.start)
        at_step(m, 7, a0.second)
        at_step(m, 9, lambda: on(0, f0.fourth))
        at_step(m, 11, lambda: on(0, f1.fourth), lambda: weight_grads(1))
        return carry

    def weight_grads(n):
        cols = lanes[n]
        for dst, src in ((ha.at[0, 0:2], gq), (ha.at[0, 2:4], gk), (ha.at[1, 0:2], gv)):
            dst[:, :, :, cols] = dot_tn(x[...], src[:, cols]).astype(BF).reshape(2, 4, BLOCK, half)

    lax.fori_loop(0, 12, step, 0)
    a1.start()
    held[0, 0:1] = jnp.sum(gq[...].astype(F32), axis=0, keepdims=True)
    held[0, 1:2] = jnp.sum(gv[...].astype(F32), axis=0, keepdims=True)
    total.start()
    a0.third()
    a1.second()
    total.hop(0)
    input_gradient(x, cot, ga_in, middle, keep, routes, gq, gk, gv, cot)
    last = bring(cot, in_grad, 3)
    last.start()
    total.hop(1)
    a0.fourth()
    a1.third()
    total.hop(2)
    f0.fifth(sf.at[0])
    f1.fifth(sf.at[1])
    square = jnp.sum(sf[...] * sf[...])
    a1.fourth()
    held[4] = total.end()
    sv[...] = jnp.zeros_like(sv)
    own_share(p, held[4], sv, 12 * width // 32)
    a0.fifth(sa.at[:, lanes[0]])
    a1.fifth(sa.at[:, lanes[1]])
    square += jnp.sum(sa[...] * sa[...]) + jnp.sum(sv[...] * sv[...])
    found = norm_sum(p, square, slots, nsend, nrecv)
    norm[...] = jnp.sqrt(found)
    for s in (f0, f1, a0, a1, total):
        s.drain()
    last.wait()


def layer_back(x, cot, normed, active, slope, factor, gf, ga, q, k, v, context, log_total, vec, lens, keep, routes):
    tokens, width = x.shape
    outs = [jax.ShapeDtypeStruct(x.shape, BF), jax.ShapeDtypeStruct(x.shape, BF), jax.ShapeDtypeStruct((2, BLOCK, width), F32),
            jax.ShapeDtypeStruct((BLOCK, width), F32), jax.ShapeDtypeStruct((8, 384), F32), jax.ShapeDtypeStruct((1, 1), F32)]
    dma = pltpu.SemaphoreType.DMA
    rows = pltpu.VMEM(x.shape, BF)
    wide = pltpu.VMEM(x.shape, F32)
    strips = pltpu.VMEM(ga.shape, BF)
    scratch = [rows, rows, wide, wide, rows, rows, pltpu.VMEM((LEN // 2, width), BF), strips, strips,
               pltpu.VMEM((4, tokens, width), BF), pltpu.VMEM((4, tokens, width), BF), pltpu.VMEM(gf.shape, BF),
               pltpu.VMEM(vec.shape, F32), pltpu.VMEM((5, ROWS, width), F32), pltpu.VMEM((6, ROWS, width), F32),
               pltpu.VMEM((32, 8, 128), F32),
               dma((11,)), dma((2,)), dma((32,)), dma((32,)), dma((6,)), dma((6,))]
    scratch += fold_scratch(width) * 2 + fold_scratch(width // 2) * 2
    vmem = pl.BlockSpec(memory_space=pltpu.VMEM)
    smem = pl.BlockSpec(memory_space=pltpu.SMEM)
    hbm = pl.BlockSpec(memory_space=pl.ANY)
    return pl.pallas_call(
        layer_back_kernel,
        out_shape=outs,
        in_specs=[hbm] * 5 + [vmem] + [hbm] * 6 + [vmem] * 2 + [smem] * 3,
        out_specs=[hbm] * 2 + [vmem] * 4,
        scratch_shapes=scratch,
        compiler_params=pltpu.CompilerParams(collective_id=1, has_side_effects=True, vmem_limit_bytes=67043328),
        name="feed_and_back",
    )(x, cot, normed, active, slope, factor, gf, ga, q, k, v, context, log_total, vec, lens, keep, routes)


def halves_of(t):
    high = t.astype(BF)
    return high, (t - high.astype(F32)).astype(BF)


def exact_dot(a, b, dims):
    dot = lambda x, y: lax.dot_general(x, y, (dims, ((), ())), preferred_element_type=F32)
    return dot(a[0], b[0]) + (dot(a[0], b[1]) + dot(a[1], b[0]))


def shampoo_block(grad, w, st, ro, mo, st_new, mo_new, w_new, b, factor):
    clipped = grad * factor
    moment = momentum_decay * mo[b] + clipped
    both = halves_of(clipped)
    left = exact_dot(both, both, ((1,), (1,)))
    right = exact_dot(both, both, ((0,), (0,)))
    st_new[b, 0] = stat_decay * st[b, 0] + (1.0 - stat_decay) * left
    st_new[b, 1] = stat_decay * st[b, 1] + (1.0 - stat_decay) * right
    mo_new[b] = moment
    turned = exact_dot(halves_of(ro[b, 0]), halves_of(moment), ((1,), (0,)))
    turned = exact_dot(halves_of(turned), halves_of(ro[b, 1]), ((1,), (0,)))
    w_new[b] = w[b] - matrix_rate * (turned + matrix_decay * w[b])


def optimizer_kernel(norm, sa, sf, sv, aw, ast, ar, am, fw, fst, fr, fm, vw, v1, v2,
                     ast_n, am_n, aw_n, fst_n, fm_n, fw_n, v1_n, v2_n, vw_n, ga, gf):
    factor = clip_bound / jnp.maximum(norm[...], clip_bound)
    g = pl.program_id(0)
    many = aw.shape[0]

    @pl.when(g == 0)
    def _():
        for b in range(8):
            ga[b] = sa[:, b * BLOCK:(b + 1) * BLOCK]
            for j in range(2):
                gf[8 * j + b] = sf[j, :, b * BLOCK:(b + 1) * BLOCK]
        size = vw.shape[0]
        clipped = (sv[0:1, 0:size] * factor)[0]
        first_new = first_decay * v1[...] + (1.0 - first_decay) * clipped
        second_new = second_decay * v2[...] + (1.0 - second_decay) * clipped * clipped
        first_hat = first_new / (1.0 - first_decay**STEP)
        second_hat = second_new / (1.0 - second_decay**STEP)
        v1_n[...] = first_new
        v2_n[...] = second_new
        vw_n[...] = vw[...] - vector_rate * first_hat / (jnp.sqrt(second_hat) + adam_floor)

    for b in range(many):
        shampoo_block(ga[g * many + b], aw, ast, ar, am, ast_n, am_n, aw_n, b, factor)
    for b in range(2 * many):
        shampoo_block(gf[g * 2 * many + b], fw, fst, fr, fm, fst_n, fm_n, fw_n, b, factor)


def optimizer(norm, sa, sf, sv, aw, ast, ar, am, fw, fst, fr, fm, vw, v1, v2):
    many = 2

    def steps(t, n):
        shape = (n,) + t.shape[1:]
        return pl.BlockSpec(shape, lambda g: (g,) + (0,) * (len(shape) - 1))

    def whole(t):
        return pl.BlockSpec(t.shape, lambda g: (0,) * t.ndim)

    like = lambda t: jax.ShapeDtypeStruct(t.shape, F32)
    args = (norm, sa, sf, sv, aw, ast, ar, am, fw, fst, fr, fm, vw, v1, v2)
    specs = [whole(t) for t in args[:4]]
    specs += [steps(t, many) for t in (aw, ast, ar, am)] + [steps(t, 2 * many) for t in (fw, fst, fr, fm)]
    specs += [whole(t) for t in (vw, v1, v2)]
    outs = (ast, am, aw, fst, fm, fw, v1, v2, vw)
    return pl.pallas_call(
        optimizer_kernel,
        out_shape=[like(t) for t in outs],
        grid=(aw.shape[0] // many,),
        in_specs=specs,
        out_specs=[steps(t, many) for t in outs[:3]] + [steps(t, 2 * many) for t in outs[3:6]] + [whole(t) for t in outs[6:]],
        scratch_shapes=[pltpu.VMEM(aw.shape, F32), pltpu.VMEM(fw.shape, F32)],
        name="optimizer",
    )(*args)


def per_device(
    inputs,
    output_gradient,
    keep,
    lengths,
    routes,
    attn_weights,
    attn_stats,
    attn_roots,
    attn_momentum,
    ffn_weights,
    ffn_stats,
    ffn_roots,
    ffn_momentum,
    vec_weights,
    vec_first,
    vec_second,
):
    slots, seq_len, width = inputs.shape
    tokens = slots * seq_len
    x = inputs.reshape(tokens, width)
    cot = output_gradient.reshape(tokens, width)
    gf, ga, vec, q, k, v, context, log_total, normed, factor, active, slope = gather_attention(attn_weights, ffn_weights, vec_weights, x, lengths)
    out, in_grad, sf, sa, sv, norm = layer_back(
        x, cot, normed, active, slope, factor, gf, ga, q, k, v, context, log_total, vec, lengths, keep, routes
    )
    rest = optimizer(
        norm, sa, sf, sv,
        attn_weights, attn_stats, attn_roots, attn_momentum,
        ffn_weights, ffn_stats, ffn_roots, ffn_momentum,
        vec_weights, vec_first, vec_second,
    )
    return (out.reshape(inputs.shape), in_grad.reshape(inputs.shape), norm.reshape(()), *rest)


def solution(mesh):
    small = mesh.shape["depth"] == 2 and mesh.shape["dp"] == 16
    return jax.shard_map(
        per_device if small else per_device_general,
        mesh=mesh,
        in_specs=(
            P(("depth", "dp"), None, None),
            P(("depth", "dp"), None, None),
            P(("depth", "dp")),
            P(("depth", "dp")),
            P(("depth", "dp")),
            P(("depth", "dp"), None, None),
            P(("depth", "dp"), None, None, None),
            P(("depth", "dp"), None, None, None),
            P(("depth", "dp"), None, None),
            P(("depth", "dp"), None, None),
            P(("depth", "dp"), None, None, None),
            P(("depth", "dp"), None, None, None),
            P(("depth", "dp"), None, None),
            P(("depth", "dp")),
            P(("depth", "dp")),
            P(("depth", "dp")),
        ),
        out_specs=(
            P(("depth", "dp"), None, None),
            P(("depth", "dp"), None, None),
            P(),
            P(("depth", "dp"), None, None, None),
            P(("depth", "dp"), None, None),
            P(("depth", "dp"), None, None),
            P(("depth", "dp"), None, None, None),
            P(("depth", "dp"), None, None),
            P(("depth", "dp"), None, None),
            P(("depth", "dp")),
            P(("depth", "dp")),
            P(("depth", "dp")),
        ),
        check_vma=False,
    )
```

profile of v0, /device:TPU:0, one launch (start us, length us, event | category | flops | bytes accessed | tf_op | source)
XLA Modules:
  0.0 236.5 jit_solution(6677413740887444028)
XLA Ops:
  0.6 90.5 %gather_attention.1 = (bf16[2,4,4,2,96,768]{5,4,3,2,1,0:T(8,128)(2,1)}, bf16[2,4,4,96,768]{4,3,2,1,0:T(8,128)(2,1)}, f32[16,768]{1,0:T(8,128)}, bf16[1024,768]{1...) custom-call(f32[8,96,96]{2,1,0:T(8,128)} %aw.3, ...), custom_call_target="tpu_custom_call" | custom-call | tf_op jit(solution)/shard_map/gather_attention/pallas_call | solution.py:784
  91.1 129.7 %feed_and_back.1 = (bf16[1024,768]{1,0:T(8,128)(2,1)}, bf16[1024,768]{1,0:T(8,128)(2,1)}, f32[2,96,768]{2,1,0:T(8,128)}, f32[96,768]{1,0:T(8,128)}, f32[8,384]{1,0:T(8,128)}, /*index=5*/f32[1,1]{1,0:T(1,128)}) custom-call(bf16[1024,768]{1,0:T(8,128)(2,1)} %bitcast.6, bf16[1024,768]{1,0:T(8,128)(2,1)} %bitcast.9, f32[1024,768]{1,0:T(8,128)} %get-tuple-element.39.normed_in, ...), custom_call_target="tpu_custom_call" | custom-call | tf_op jit(solution)/shard_map/feed_and_back/pallas_call | solution.py:1184
  220.9 0.0 copy-start.1
  220.9 10.7 %optimizer.1 = (f32[8,2,96,96]{3,2,1,0:T(8,128)}, f32[8,96,96]{2,1,0:T(8,128)}, f32[8,96,96]{2,1,0:T(8,128)}, f32[16,2,96,96]{3,2,1,0:T(8,128)}, f32[16,96,96]{2...) custom-call(f32[1,1]{1,0:T(1,128)} %get-tuple-element.53.norm, ...), custom_call_target="tpu_custom_call" | custom-call | tf_op jit(solution)/shard_map/optimizer/pallas_call | solution.py:1263
  231.6 0.0 copy-done.1
  231.6 0.0 copy-start
  231.6 1.1 copy.31
  232.7 0.8 copy-done
  233.6 1.1 copy.32
Async XLA Ops:
  220.9 10.7 %copy-start.1 = (bf16[1024,768]{1,0:T(8,128)(2,1)S(1)}, bf16[1024,768]{1,0:T(8,128)(2,1)}, u32[]{:S(2)}) copy-start(bf16[1024,768]{1,0:T(8,128)(2,1)} %get-tuple-element.51) | copy-start | bytes 4718596
  231.6 2.0 copy-start
where the time goes:
time: 237 us
  Pallas kernels  231 us (97%)
  local copies, waits for them, and re-layouts  3.11 us (1%)
  between operations  2.51 us (1%)
    pallas_call x1, Pallas kernels, layer_back(): pl.pallas_call(layer_back_kernel, out_shape=outs, in_specs=[hbm] * 5 + [v...  130 us
    pallas_call x1, Pallas kernels, gather_attention(): pl.pallas_call(gather_attention_kernel, out_shape=outs, in_specs=[vmem] *...  90.5 us
    pallas_call x1, Pallas kernels, optimizer(): pl.pallas_call(optimizer_kernel, out_shape=[like(t) for t in outs], grid=...  10.7 us

commit v1 on v0

--- a/solution.py
+++ b/solution.py
@@ -800,7 +800,7 @@
     shape = (BLOCK, width)
     return [pltpu.VMEM((4, 4) + shape, BF), pltpu.VMEM((4,) + shape, BF), pltpu.VMEM((4,) + shape, BF),
             pltpu.VMEM((4,) + shape, BF), pltpu.VMEM((3,) + shape, BF),
-            pltpu.SemaphoreType.DMA((7,)), pltpu.SemaphoreType.DMA((7,))]
+            pltpu.SemaphoreType.DMA((10,)), pltpu.SemaphoreType.DMA((10,))]
 
 
 class Total(Mail):
@@ -897,10 +897,16 @@
         self.p, self.home, self.pair, self.diag, self.flat, self.late, self.line = p, home, pair, diag, flat, late, line
         self.ca, self.cb = a % 4, b % 4
         d, z, c = p["d"], p["z"], p["c"]
-        pieces = [(away, pair, (1 - d, p["i"])), (pair.at[:, p["cd"]], diag, (d, b)), (pair.at[:, self.cb], flat, (d, b)),
+        self.away, self.send, self.recv, self.core = away, send, recv, (1 - d, p["i"])
+        pieces = [(pair.at[:, p["cd"]], diag, (d, b)), (pair.at[:, self.cb], flat, (d, b)),
                   (pair.at[:, self.ca], late, (d, a))]
         pieces += [(pair.at[(z + k) % 4, c], line.at[k - 1], (d, ((z + k) % 4) * 4 + c)) for k in (1, 2, 3)]
-        self.copies = [remote(src, dst, send, recv, n, dev) for n, (src, dst, dev) in enumerate(pieces)]
+        self.copies = [None] + [remote(src, dst, send, recv, n, dev) for n, (src, dst, dev) in enumerate(pieces)]
+
+    def part(self, z):
+        return pltpu.make_async_remote_copy(
+            src_ref=self.away.at[z], dst_ref=self.pair.at[z], send_sem=self.send.at[6 + z], recv_sem=self.recv.at[6 + z],
+            device_id=self.core, device_id_type=MESH)
 
     def add(self, dst, *others):
         total = dst[...].astype(F32)
@@ -908,11 +914,18 @@
             total += o[...].astype(F32)
         dst[...] = total.astype(dst.dtype)
 
+    def column_part(self, c):
+        return pltpu.make_async_remote_copy(
+            src_ref=self.away.at[:, c], dst_ref=self.pair.at[:, c], send_sem=self.send.at[6 + c], recv_sem=self.recv.at[6 + c],
+            device_id=self.core, device_id_type=MESH)
+
     def start(self):
-        self.copies[0].start()
+        for z in range(4):
+            self.part(z).start()
 
     def second(self):
-        self.copies[0].wait_recv()
+        for z in range(4):
+            self.part(z).wait_recv()
         for col, n in ((self.p["cd"], 1), (self.cb, 2)):
             self.add(self.pair.at[:, col], self.home.at[:, col])
             self.copies[n].start()
@@ -943,7 +956,7 @@
         out[...] = total
 
     def drain(self):
-        for copy in self.copies:
+        for copy in self.copies[1:] + [self.part(z) for z in range(4)]:
             copy.wait_send()
 
 
@@ -961,23 +974,25 @@
     def bring(src, dst, n):
         return pltpu.make_async_copy(src, dst, load.at[n])
 
-    ahead = [bring(active_in, active, 0), bring(normed_in, normed, 1), bring(x_in, x, 2), bring(cot_in, cot, 9)]
-    slopes = bring(slope_in, slope, 10)
+    quarters = [bring(active_in.at[q], active.at[q], q) for q in range(4)]
+    others = [bring(normed_in, normed, 4), bring(x_in, x, 5), bring(cot_in, cot, 6)]
+    slopes = bring(slope_in, slope, 7)
 
     def fetch_down(t, carry):
         q, s = t // 8, t % 8
-        pltpu.make_async_copy(gf.at[1, q, s // 2, s % 2], w2.at[q // 2, 2 * (q % 2) + s // 4, s % 4], wload.at[0]).start()
+        pltpu.make_async_copy(gf.at[1, q, s // 2, s % 2], w2.at[q // 2, 2 * (q % 2) + s // 4, s % 4], wload.at[q]).start()
         return carry
 
     def fetch(t, carry):
         q, s = t // 8, t % 8
         pltpu.make_async_copy(gf.at[0, s // 2, 2 * (s % 2) + q // 2, q % 2], w1.at[q // 2, 2 * (q % 2) + s // 4, s % 4],
-                              wload.at[1]).start()
-        return carry
-
-    ahead[0].start()
-    lax.fori_loop(0, 32, fetch_down, 0)
-    for copy in ahead[1:]:
+                              wload.at[4]).start()
+        return carry
+
+    for q in range(4):
+        quarters[q].start()
+        lax.fori_loop(8 * q, 8 * q + 8, fetch_down, 0)
+    for copy in others:
         copy.start()
     slopes.start()
     lax.fori_loop(0, 32, fetch, 0)
@@ -997,26 +1012,27 @@
     def add_vec(n, value):
         gvec[n:n + 1] += value
 
-    def lower(s, carry):
-        rows = seq_rows(s)
-        low[rows] = (normed[rows] * vec_part(vec, 8) + vec_part(vec, 9)).astype(BF)
-        return carry
-
-    for copy in ahead[1:2]:
-        copy.wait()
-    lax.fori_loop(0, seqs, lower, 0)
-    pltpu.make_async_copy(w2, w2, wload.at[0]).wait()
-    for copy in ahead[:1] + ahead[2:]:
+    for q in range(4):
+        quarters[q].wait()
+        pltpu.make_async_copy(quarter(w2, q), quarter(w2, q), wload.at[q]).wait()
+
+        def gain(s, carry):
+            rows = seq_rows(s)
+            found = dot_nn(active[q, rows], square_of(quarter(w2, q)[...]))
+            middle[rows] = found if q == 0 else middle[rows] + found
+            return carry
+
+        lax.fori_loop(0, seqs, gain, 0)
+    for copy in others:
         copy.wait()
     tile = LEN // 2
 
     def leave(t, carry):
         rows = tile_rows(t, tile)
-        show = pltpu.make_async_copy(image, out.at[rows], load.at[3])
-        branch = dot_nn(active[0, rows], square_of(quarter(w2, 0)[...]))
-        for q in range(1, 4):
-            branch += dot_nn(active[q, rows], square_of(quarter(w2, q)[...]))
-        resid = normed[rows] * vec_part(vec, 8) + vec_part(vec, 9) + (branch + vec_part(vec, 7))
+        show = pltpu.make_async_copy(image, out.at[rows], load.at[14])
+        hidden = normed[rows] * vec_part(vec, 8) + vec_part(vec, 9)
+        low[rows] = hidden.astype(BF)
+        resid = hidden + (middle[rows] + vec_part(vec, 7))
         center = resid - mean_of(resid)
         scale = lax.rsqrt(mean_of(center * center) + norm_floor)
         second = center * scale
@@ -1036,16 +1052,17 @@
         return carry
 
     lax.fori_loop(0, 2 * seqs, leave, 0)
+    meet_all()
+
     def down_grad(t, carry):
         q, h = t // 2, t % 2
         found = dot_tn(active[q, :, pl.ds(pl.multiple_of(h * half, half), half)], grad_low[...])
         hf[1, q, pl.ds(2 * h, 2)] = found.astype(BF).reshape(2, 2, BLOCK, width)
+        at_step(h, 1, lambda: on(0, lambda: f0.part(q).start(), lambda: f1.part(q).start()))
         return carry
 
     lax.fori_loop(0, 8, down_grad, 0)
-    meet_all()
-    on(0, f0.start, f1.start)
-    again = [bring(src, slope.at[n], 4 + n) for n, src in enumerate((context_in, q_in, k_in, v_in))]
+    again = [bring(src, slope.at[n], 8 + n) for n, src in enumerate((context_in, q_in, k_in, v_in))]
     context, qs, ks, vs = (slope.at[n] for n in range(4))
     slopes.wait()
 
@@ -1065,17 +1082,19 @@
 
         lax.fori_loop(0, seqs, part, 0)
         lax.fori_loop(0, 2, up_grad, 0)
-        at_step(q, 1, lambda: on(1, f0.second))
-        at_step(q, 2, lambda: on(1, f1.second))
+        at_step(q, 0, lambda: on(1, f0.second, f1.second))
+        for j, f in enumerate((f0, f1)):
+            at_step(q % 2, j, lambda f=f: on(1, lambda: f.column_part(q // 2).start(), lambda: f.column_part(2 + q // 2).start()))
+        at_step(q, 2, lambda: on(1, f0.third))
+        at_step(q, 3, lambda: on(1, f1.third))
         return carry
 
     lax.fori_loop(0, 4, turn, 0)
     for copy in again:
         copy.start()
-    pltpu.make_async_copy(w1, w1, wload.at[1]).wait()
-    square_in = bring(ga, ga_in, 8)
+    pltpu.make_async_copy(w1, w1, wload.at[4]).wait()
+    square_in = bring(ga, ga_in, 12)
     square_in.start()
-    on(1, f0.start, f1.start)
 
     def close(t, carry):
         rows = tile_rows(t, tile)
@@ -1092,10 +1111,10 @@
         return carry
 
     lax.fori_loop(0, seqs, close, 0)
-    on(1, f0.third)
+    on(0, f0.second)
     lax.fori_loop(seqs, 2 * seqs, close, 0)
-    on(1, f1.third)
-    on(0, f0.second)
+    on(1, f0.fourth)
+    on(0, f1.second)
     gq, gk, gv, grad_context = (active.at[n] for n in range(4))
     square_in.wait()
     again[0].wait()
@@ -1110,21 +1129,20 @@
     held[0, 2:3] = jnp.sum(grad_low[...].astype(F32), axis=0, keepdims=True)
     for h in range(2):
         ha[1, 2 + h] = dot_tn(context[:, h * half:(h + 1) * half], grad_low[...]).astype(BF).reshape(4, BLOCK, width)
-    on(0, f1.second)
+    on(1, f1.fourth)
     for copy in again[1:]:
         copy.wait()
 
     def step(m, carry):
         n = ((m % 6) // 3) * 6 + (m // 6) * 3 + m % 3
         attend_back(n, qs, ks, vs, grad_context, log_total, lens, gq, gk, gv)
-        at_step(m, 1, lambda: on(1, f0.fourth))
-        at_step(m, 2, lambda: on(1, f1.fourth))
-        at_step(m, 3, lambda: on(0, f0.third))
-        at_step(m, 4, lambda: on(0, f1.third))
-        at_step(m, 5, lambda: weight_grads(0), a0.start)
+        at_step(m, 0, lambda: on(0, f0.third))
+        at_step(m, 1, lambda: on(0, f1.third))
+        at_step(m, 5, lambda: weight_grads(0), a0.start, lambda: on(0, f0.fourth))
+        at_step(m, 6, lambda: on(0, f1.fourth))
         at_step(m, 7, a0.second)
-        at_step(m, 9, lambda: on(0, f0.fourth))
-        at_step(m, 11, lambda: on(0, f1.fourth), lambda: weight_grads(1))
+        at_step(m, 10, a0.third)
+        at_step(m, 11, lambda: weight_grads(1))
         return carry
 
     def weight_grads(n):
@@ -1137,15 +1155,14 @@
     held[0, 0:1] = jnp.sum(gq[...].astype(F32), axis=0, keepdims=True)
     held[0, 1:2] = jnp.sum(gv[...].astype(F32), axis=0, keepdims=True)
     total.start()
-    a0.third()
     a1.second()
+    a0.fourth()
     total.hop(0)
     input_gradient(x, cot, ga_in, middle, keep, routes, gq, gk, gv, cot)
-    last = bring(cot, in_grad, 3)
+    last = bring(cot, in_grad, 13)
     last.start()
+    a1.third()
     total.hop(1)
-    a0.fourth()
-    a1.third()
     total.hop(2)
     f0.fifth(sf.at[0])
     f1.fifth(sf.at[1])
@@ -1176,7 +1193,7 @@
                pltpu.VMEM((4, tokens, width), BF), pltpu.VMEM((4, tokens, width), BF), pltpu.VMEM(gf.shape, BF),
                pltpu.VMEM(vec.shape, F32), pltpu.VMEM((5, ROWS, width), F32), pltpu.VMEM((6, ROWS, width), F32),
                pltpu.VMEM((32, 8, 128), F32),
-               dma((11,)), dma((2,)), dma((32,)), dma((32,)), dma((6,)), dma((6,))]
+               dma((15,)), dma((5,)), dma((32,)), dma((32,)), dma((6,)), dma((6,))]
     scratch += fold_scratch(width) * 2 + fold_scratch(width // 2) * 2
     vmem = pl.BlockSpec(memory_space=pltpu.VMEM)
     smem = pl.BlockSpec(memory_space=pltpu.SMEM)
@@ -1216,11 +1233,13 @@
     w_new[b] = w[b] - matrix_rate * (turned + matrix_decay * w[b])
 
 
-def optimizer_kernel(norm, sa, sf, sv, aw, ast, ar, am, fw, fst, fr, fm, vw, v1, v2,
-                     ast_n, am_n, aw_n, fst_n, fm_n, fw_n, v1_n, v2_n, vw_n, ga, gf):
+def optimizer_kernel(norm, sa, sf, sv, aw, ast, ar, am, fw, fst, fr, fm, vw, v1, v2, rows, grads,
+                     rows_n, grads_n, ast_n, am_n, aw_n, fst_n, fm_n, fw_n, v1_n, v2_n, vw_n, ga, gf):
     factor = clip_bound / jnp.maximum(norm[...], clip_bound)
     g = pl.program_id(0)
     many = aw.shape[0]
+    rows_n[...] = rows[...]
+    grads_n[...] = grads[...]
 
     @pl.when(g == 0)
     def _():
@@ -1244,7 +1263,7 @@
         shampoo_block(gf[g * 2 * many + b], fw, fst, fr, fm, fst_n, fm_n, fw_n, b, factor)
 
 
-def optimizer(norm, sa, sf, sv, aw, ast, ar, am, fw, fst, fr, fm, vw, v1, v2):
+def optimizer(norm, sa, sf, sv, aw, ast, ar, am, fw, fst, fr, fm, vw, v1, v2, rows, grads):
     many = 2
 
     def steps(t, n):
@@ -1254,18 +1273,20 @@
     def whole(t):
         return pl.BlockSpec(t.shape, lambda g: (0,) * t.ndim)
 
-    like = lambda t: jax.ShapeDtypeStruct(t.shape, F32)
-    args = (norm, sa, sf, sv, aw, ast, ar, am, fw, fst, fr, fm, vw, v1, v2)
+    like = lambda t: jax.ShapeDtypeStruct(t.shape, t.dtype)
+    args = (norm, sa, sf, sv, aw, ast, ar, am, fw, fst, fr, fm, vw, v1, v2, rows, grads)
+    part = rows.shape[0] * many // aw.shape[0]
     specs = [whole(t) for t in args[:4]]
     specs += [steps(t, many) for t in (aw, ast, ar, am)] + [steps(t, 2 * many) for t in (fw, fst, fr, fm)]
-    specs += [whole(t) for t in (vw, v1, v2)]
-    outs = (ast, am, aw, fst, fm, fw, v1, v2, vw)
+    specs += [whole(t) for t in (vw, v1, v2)] + [steps(t, part) for t in (rows, grads)]
+    outs = (rows, grads, ast, am, aw, fst, fm, fw, v1, v2, vw)
     return pl.pallas_call(
         optimizer_kernel,
         out_shape=[like(t) for t in outs],
         grid=(aw.shape[0] // many,),
         in_specs=specs,
-        out_specs=[steps(t, many) for t in outs[:3]] + [steps(t, 2 * many) for t in outs[3:6]] + [whole(t) for t in outs[6:]],
+        out_specs=[steps(t, part) for t in outs[:2]] + [steps(t, many) for t in outs[2:5]] + [steps(t, 2 * many) for t in outs[5:8]]
+        + [whole(t) for t in outs[8:]],
         scratch_shapes=[pltpu.VMEM(aw.shape, F32), pltpu.VMEM(fw.shape, F32)],
         name="optimizer",
     )(*args)
@@ -1297,11 +1318,11 @@
     out, in_grad, sf, sa, sv, norm = layer_back(
         x, cot, normed, active, slope, factor, gf, ga, q, k, v, context, log_total, vec, lengths, keep, routes
     )
-    rest = optimizer(
+    out, in_grad, *rest = optimizer(
         norm, sa, sf, sv,
         attn_weights, attn_stats, attn_roots, attn_momentum,
         ffn_weights, ffn_stats, ffn_roots, ffn_momentum,
-        vec_weights, vec_first, vec_second,
+        vec_weights, vec_first, vec_second, out, in_grad,
     )
     return (out.reshape(inputs.shape), in_grad.reshape(inputs.shape), norm.reshape(()), *rest)
 

time: 237 us -> 228 us (0.962)
  Pallas kernels: 231 us -> 226 us
  local copies, waits for them, and re-layouts: 3.11 us -> 0 us
    pallas_call x1, Pallas kernels: 130 us -> 124 us  [layer_back(): pl.pallas_call(layer_back_kernel, out_shape=outs, in_specs=[hbm] * 5 + [v...]
    unnamed x6 -> x0, local copies, waits for them, and re-layouts: 3.11 us -> none
where the time goes in v1:
time: 228 us
  Pallas kernels  226 us (99%)
  between operations  2.4 us (1%)
    pallas_call x1, Pallas kernels, layer_back(): pl.pallas_call(layer_back_kernel, out_shape=outs, in_specs=[hbm] * 5 + [v...  124 us
    pallas_call x1, Pallas kernels, gather_attention(): pl.pallas_call(gather_attention_kernel, out_shape=outs, in_specs=[vmem] *...  90.5 us
    pallas_call x1, Pallas kernels, optimizer(): pl.pallas_call(optimizer_kernel, out_shape=[like(t) for t in outs], grid=...  11.7 us

profile of v1, /device:TPU:0, one launch (start us, length us, event | category | flops | bytes accessed | tf_op | source)
XLA Modules:
  0.0 228.0 jit_solution(2687721664785873498)
XLA Ops:
  0.6 90.5 %gather_attention.1 = (bf16[2,4,4,2,96,768]{5,4,3,2,1,0:T(8,128)(2,1)}, bf16[2,4,4,96,768]{4,3,2,1,0:T(8,128)(2,1)}, f32[16,768]{1,0:T(8,128)}, bf16[1024,768]{1...) custom-call(f32[8,96,96]{2,1,0:T(8,128)} %aw.3, ...), custom_call_target="tpu_custom_call" | custom-call | tf_op jit(solution)/shard_map/gather_attention/pallas_call | solution.py:784
  91.1 123.5 %feed_and_back.1 = (bf16[1024,768]{1,0:T(8,128)(2,1)}, bf16[1024,768]{1,0:T(8,128)(2,1)}, f32[2,96,768]{2,1,0:T(8,128)}, f32[96,768]{1,0:T(8,128)}, f32[8,384]{1,0:T(8,128)}, /*index=5*/f32[1,1]{1,0:T(1,128)}) custom-call(bf16[1024,768]{1,0:T(8,128)(2,1)} %bitcast.6, bf16[1024,768]{1,0:T(8,128)(2,1)} %bitcast.7, f32[1024,768]{1,0:T(8,128)} %get-tuple-element.41.normed_in, ...), custom_call_target="tpu_custom_call" | custom-call | tf_op jit(solution)/shard_map/feed_and_back/pallas_call | solution.py:1201
  214.6 11.7 %optimizer.1 = (bf16[1024,768]{1,0:T(8,128)(2,1)}, bf16[1024,768]{1,0:T(8,128)(2,1)}, f32[8,2,96,96]{3,2,1,0:T(8,128)}, f32[8,96,96]{2,1,0:T(8,128)}, f32[8,96,9...) custom-call(f32[1,1]{1,0:T(1,128)} %get-tuple-element.53.norm, ...), custom_call_target="tpu_custom_call" | custom-call | tf_op jit(solution)/shard_map/optimizer/pallas_call | solution.py:1283

commit v2 on v1

--- a/solution.py
+++ b/solution.py
@@ -642,7 +642,7 @@
     return vec[n:n + 1]
 
 
-def input_gradient(x, cot, ga, grad_resid, keep, routes, gq, gk, gv, in_grad):
+def input_gradient(x, cot, ga, grad_resid, keep, routes, gq, gk, gv, in_grad, first, last):
     def tile(s, carry):
         rows = tile_rows(s, LEN // 2)
         total = grad_resid[rows] + dot_nt(gq[rows], square_of(ga[0, 0:2]))
@@ -651,7 +651,7 @@
         in_grad[rows] = jnp.where(served_flag(keep, routes, s // 2) > 0, total.astype(BF), cot[rows])
         return carry
 
-    lax.fori_loop(0, 2 * x.shape[0] // LEN, tile, 0)
+    lax.fori_loop(first, last, tile, 0)
 
 
 def gather_attention_kernel(aw, fw, vw, x, lens, gf, ga_out, vec, q_out, k_out, v_out, context_out, log_total, normed_out, factor,
@@ -1155,14 +1155,15 @@
     held[0, 0:1] = jnp.sum(gq[...].astype(F32), axis=0, keepdims=True)
     held[0, 1:2] = jnp.sum(gv[...].astype(F32), axis=0, keepdims=True)
     total.start()
+    input_gradient(x, cot, ga_in, middle, keep, routes, gq, gk, gv, cot, 0, seqs)
     a1.second()
+    total.hop(0)
     a0.fourth()
-    total.hop(0)
-    input_gradient(x, cot, ga_in, middle, keep, routes, gq, gk, gv, cot)
+    input_gradient(x, cot, ga_in, middle, keep, routes, gq, gk, gv, cot, seqs, 2 * seqs)
+    total.hop(1)
     last = bring(cot, in_grad, 13)
     last.start()
     a1.third()
-    total.hop(1)
     total.hop(2)
     f0.fifth(sf.at[0])
     f1.fifth(sf.at[1])

time: 228 us -> 229 us (level)
  no operation moved by 1% of the time
where the time goes in v2:
time: 229 us
  Pallas kernels  226 us (99%)
  between operations  2.4 us (1%)
    pallas_call x1, Pallas kernels, layer_back(): pl.pallas_call(layer_back_kernel, out_shape=outs, in_specs=[hbm] * 5 + [v...  124 us
    pallas_call x1, Pallas kernels, gather_attention(): pl.pallas_call(gather_attention_kernel, out_shape=outs, in_specs=[vmem] *...  90.5 us
    pallas_call x1, Pallas kernels, optimizer(): pl.pallas_call(optimizer_kernel, out_shape=[like(t) for t in outs], grid=...  11.7 us

profile of v2, /device:TPU:0, one launch (start us, length us, event | category | flops | bytes accessed | tf_op | source)
XLA Modules:
  0.0 228.7 jit_solution(7001691748864807581)
XLA Ops:
  0.6 90.5 %gather_attention.1 = (bf16[2,4,4,2,96,768]{5,4,3,2,1,0:T(8,128)(2,1)}, bf16[2,4,4,96,768]{4,3,2,1,0:T(8,128)(2,1)}, f32[16,768]{1,0:T(8,128)}, bf16[1024,768]{1...) custom-call(f32[8,96,96]{2,1,0:T(8,128)} %aw.3, ...), custom_call_target="tpu_custom_call" | custom-call | tf_op jit(solution)/shard_map/gather_attention/pallas_call | solution.py:784
  91.1 124.2 %feed_and_back.1 = (bf16[1024,768]{1,0:T(8,128)(2,1)}, bf16[1024,768]{1,0:T(8,128)(2,1)}, f32[2,96,768]{2,1,0:T(8,128)}, f32[96,768]{1,0:T(8,128)}, f32[8,384]{1,0:T(8,128)}, /*index=5*/f32[1,1]{1,0:T(1,128)}) custom-call(bf16[1024,768]{1,0:T(8,128)(2,1)} %bitcast.6, bf16[1024,768]{1,0:T(8,128)(2,1)} %bitcast.7, f32[1024,768]{1,0:T(8,128)} %get-tuple-element.41.normed_in, ...), custom_call_target="tpu_custom_call" | custom-call | tf_op jit(solution)/shard_map/feed_and_back/pallas_call | solution.py:1202
  215.3 11.7 %optimizer.1 = (bf16[1024,768]{1,0:T(8,128)(2,1)}, bf16[1024,768]{1,0:T(8,128)(2,1)}, f32[8,2,96,96]{3,2,1,0:T(8,128)}, f32[8,96,96]{2,1,0:T(8,128)}, f32[8,96,9...) custom-call(f32[1,1]{1,0:T(1,128)} %get-tuple-element.53.norm, ...), custom_call_target="tpu_custom_call" | custom-call | tf_op jit(solution)/shard_map/optimizer/pallas_call | solution.py:1284

commit v3 on v1

--- a/solution.py
+++ b/solution.py
@@ -1264,7 +1264,7 @@
 
 
 def optimizer(norm, sa, sf, sv, aw, ast, ar, am, fw, fst, fr, fm, vw, v1, v2, rows, grads):
-    many = 2
+    many = 1
 
     def steps(t, n):
         shape = (n,) + t.shape[1:]

time: 228 us -> 230 us (level)
  no operation moved by 1% of the time
where the time goes in v3:
time: 230 us; the launch traced here: 229 us
  Pallas kernels  227 us (99%)
  between operations  2.4 us (1%)
    pallas_call x1, Pallas kernels, layer_back(): pl.pallas_call(layer_back_kernel, out_shape=outs, in_specs=[hbm] * 5 + [v...  124 us
    pallas_call x1, Pallas kernels, gather_attention(): pl.pallas_call(gather_attention_kernel, out_shape=outs, in_specs=[vmem] *...  90.5 us
    pallas_call x1, Pallas kernels, optimizer(): pl.pallas_call(optimizer_kernel, out_shape=[like(t) for t in outs], grid=...  13 us

profile of v3, /device:TPU:0, one launch (start us, length us, event | category | flops | bytes accessed | tf_op | source)
XLA Modules:
  0.0 229.3 jit_solution(13553552384591944576)
XLA Ops:
  0.6 90.5 %gather_attention.1 = (bf16[2,4,4,2,96,768]{5,4,3,2,1,0:T(8,128)(2,1)}, bf16[2,4,4,96,768]{4,3,2,1,0:T(8,128)(2,1)}, f32[16,768]{1,0:T(8,128)}, bf16[1024,768]{1...) custom-call(f32[8,96,96]{2,1,0:T(8,128)} %aw.3, ...), custom_call_target="tpu_custom_call" | custom-call | tf_op jit(solution)/shard_map/gather_attention/pallas_call | solution.py:784
  91.1 123.5 %feed_and_back.1 = (bf16[1024,768]{1,0:T(8,128)(2,1)}, bf16[1024,768]{1,0:T(8,128)(2,1)}, f32[2,96,768]{2,1,0:T(8,128)}, f32[96,768]{1,0:T(8,128)}, f32[8,384]{1,0:T(8,128)}, /*index=5*/f32[1,1]{1,0:T(1,128)}) custom-call(bf16[1024,768]{1,0:T(8,128)(2,1)} %bitcast.6, bf16[1024,768]{1,0:T(8,128)(2,1)} %bitcast.7, f32[1024,768]{1,0:T(8,128)} %get-tuple-element.41.normed_in, ...), custom_call_target="tpu_custom_call" | custom-call | tf_op jit(solution)/shard_map/feed_and_back/pallas_call | solution.py:1201
  214.6 13.0 %optimizer.1 = (bf16[1024,768]{1,0:T(8,128)(2,1)}, bf16[1024,768]{1,0:T(8,128)(2,1)}, f32[8,2,96,96]{3,2,1,0:T(8,128)}, f32[8,96,96]{2,1,0:T(8,128)}, f32[8,96,9...) custom-call(f32[1,1]{1,0:T(1,128)} %get-tuple-element.53.norm, ...), custom_call_target="tpu_custom_call" | custom-call | tf_op jit(solution)/shard_map/optimizer/pallas_call | solution.py:1283
